TPU v7x, 32 devices: a whole 2x2x4 slice. The times are simulated.
32 devices in a mesh: col: 16 (over z, x, core), row: 2 (over y).
Axes of the slice: x: 2, y: 2, z: 4, core: 2. Of those that a mesh axis runs over, the one named last changes fastest.
Arguments:
- uniq_rows: bfloat16 [32, 128, 1536], P('row', 'col'), may hold values from -6 to 6
- row_ids: int32 [32, 128, 8], P('row', 'col'), may hold values from 0 to 255, as said below
- sample_idx: int32 [512, 128], P('row', 'col'), may hold values from 0 to 7, as said below
- fm_proj: bfloat16 [128, 8], replicated, may hold values from -0.5 to 0.5
- ln_gain: float32 [1024], replicated, may hold values from 0.5 to 1.5
- w_up: bfloat16 [1024, 2048], P(None, 'row'), may hold values from -0.1875 to 0.1875
- w_down: bfloat16 [2048, 1536], P('row'), may hold values from -0.125 to 0.125
- w_lc: bfloat16 [8, 128], replicated, may hold values from -0.5 to 0.5
- w_res: bfloat16 [16, 128], replicated, may hold values from -0.5 to 0.5
- out_gain: float32 [192], replicated, may hold values from 0.5 to 1.5
- cotangent: bfloat16 [512, 3072], P(('row', 'col')), may hold values from -6 to 6
- moment1: float32 [128, 256, 192], P('col', 'row'), may hold values from -1.5 to 1.5
- moment2: float32 [128, 256], P('col', 'row'), may hold values from 0.01 to 0.1
Outputs:
- layer_out: bfloat16 [512, 3072], P(('row', 'col'))
- new_moment1: float32 [128, 256, 192], P('col', 'row')
- new_moment2: float32 [128, 256], P('col', 'row')
- row_step: float32 [128, 256, 192], P('col', 'row')
Inputs may be any that keep to these rules, and one draw needn't show every extreme that they name: `sample_idx`: for each block of 16 samples and each slot, every one of the 8 list entries is used by at least one sample of the block. `row_ids`: the 8 ids of one list are distinct. Row v of a slot is owned by index v // 128 of row. Of the 1024 list entries held by one device (the blocks of its index of row, the slots of its index of col), at most 640 name rows of one owner, and in every draw some owner is named exactly 640 times on each device.
All inputs are finite; a program needn't handle non-finite values.
Results may differ from a plain program's by a relative error of at most 0.005.
Values may be sent and summed in bfloat16 or wider, within the bound.
A program may use at most 64 MiB of HBM per device.

v0:
```python
import jax
import jax.numpy as jnp
from jax import lax
from jax.sharding import PartitionSpec as P

HIGH = lax.Precision.HIGHEST


def layer_norm(values, gain):
    centered = values - jnp.mean(values, -1, keepdims=True)
    inverse = lax.rsqrt(jnp.mean(centered * centered, -1, keepdims=True) + 1e-05)
    normed = centered * inverse
    return (normed * gain, normed, inverse)


def norm_back(grad_out, normed, inverse):
    first = jnp.mean(grad_out, -1, keepdims=True)
    second = jnp.mean(grad_out * normed, -1, keepdims=True)
    return (grad_out - first - normed * second) * inverse


def silu_grad(values):
    sigma = jax.nn.sigmoid(values)
    return sigma * (1.0 + values * (1.0 - sigma))


def body(
    uniq_rows,
    row_ids,
    sample_idx,
    fm_proj,
    ln_gain,
    w_up,
    w_down,
    w_lc,
    w_res,
    out_gain,
    cotangent,
    moment1,
    moment2,
):
    columns = lax.axis_size("col")
    owners = lax.axis_size("row")
    slot_dev = uniq_rows.shape[1]
    width = out_gain.shape[0]
    uniq = uniq_rows.shape[2] // width
    samples = cotangent.shape[0]
    slots = slot_dev * columns
    vocab_dev = moment2.shape[1]
    rank = fm_proj.shape[1]
    fm_rows = w_down.shape[1] // width
    out_rows = w_res.shape[0]
    entry_iota = jnp.arange(uniq, dtype=jnp.int32)
    index_local = sample_idx.reshape(columns, samples, slot_dev)
    index = lax.all_to_all(index_local, "col", split_axis=0, concat_axis=2, tiled=True).reshape(
        samples, slots
    )
    picker = (index[:, :, None] == entry_iota).astype(jnp.bfloat16)
    moved = lax.all_to_all(uniq_rows, "col", split_axis=0, concat_axis=1, tiled=True)
    table = moved.reshape(slots, uniq, width)
    embed = jnp.einsum("stl,tle->ste", picker, table, preferred_element_type=jnp.float32).astype(
        jnp.bfloat16
    )
    compress = jnp.einsum("ste,tk->sek", embed, fm_proj, preferred_element_type=jnp.float32).astype(
        jnp.bfloat16
    )
    gram = jnp.einsum("ste,sek->stk", embed, compress, preferred_element_type=jnp.float32)
    flat = gram.reshape(samples, slots * rank)
    scaled, normed_in, inverse_in = layer_norm(flat, ln_gain)
    normal_in = scaled.astype(jnp.bfloat16)
    hidden_pre = jnp.dot(
        lax.all_gather(normal_in, "row", axis=0, tiled=True),
        w_up,
        preferred_element_type=jnp.float32,
    )
    hidden = jax.nn.silu(hidden_pre).astype(jnp.bfloat16)
    part_rows = hidden
    fm_out = lax.psum_scatter(
        jnp.dot(part_rows, w_down, preferred_element_type=jnp.float32),
        "row",
        scatter_dimension=0,
        tiled=True,
    )
    linear = jnp.einsum("lt,ste->sle", w_lc, embed, preferred_element_type=jnp.float32)
    joined = jnp.concatenate([fm_out.reshape(samples, fm_rows, width), linear], 1)
    normed_out, normed_rows, inverse_rows = layer_norm(joined, out_gain)
    residual = jnp.einsum("ot,ste->soe", w_res, embed, preferred_element_type=jnp.float32)
    layer_out = (normed_out + residual).reshape(samples, out_rows * width).astype(jnp.bfloat16)
    upstream = cotangent.astype(jnp.float32).reshape(samples, out_rows, width)
    grad_joined = norm_back(upstream * out_gain, normed_rows, inverse_rows)
    grad_fm = grad_joined[:, :fm_rows].reshape(samples, fm_rows * width).astype(jnp.bfloat16)
    grad_hidden = lax.dot_general(
        lax.all_gather(grad_fm, "row", axis=0, tiled=True),
        w_down,
        (((1,), (1,)), ((), ())),
        preferred_element_type=jnp.float32,
    )
    grad_pre = (grad_hidden * silu_grad(hidden_pre)).astype(jnp.bfloat16)
    part_rows = grad_pre
    grad_flat = lax.psum_scatter(
        lax.dot_general(
            part_rows, w_up, (((1,), (1,)), ((), ())), preferred_element_type=jnp.float32
        ).astype(jnp.bfloat16),
        "row",
        scatter_dimension=0,
        tiled=True,
    ).astype(jnp.float32)
    grad_gram = norm_back(grad_flat * ln_gain, normed_in, inverse_in).reshape(samples, slots, rank)
    grad_embed = jnp.einsum("stk,sek->ste", grad_gram, compress.astype(jnp.float32), precision=HIGH)
    grad_comp = jnp.einsum(
        "ste,stk->sek", embed, grad_gram, precision=HIGH, preferred_element_type=jnp.float32
    )
    grad_embed = grad_embed + jnp.einsum(
        "tk,sek->ste", fm_proj.astype(jnp.float32), grad_comp, precision=HIGH
    )
    grad_embed = grad_embed + jnp.einsum(
        "lt,sle->ste", w_lc.astype(jnp.float32), grad_joined[:, fm_rows:], precision=HIGH
    )
    grad_embed = grad_embed + jnp.einsum(
        "ot,soe->ste", w_res.astype(jnp.float32), upstream, precision=HIGH
    )
    list_grads = jnp.einsum("stl,ste->tle", picker.astype(jnp.float32), grad_embed, precision=HIGH)
    returned = lax.all_to_all(
        list_grads.reshape(columns, slot_dev, uniq * width),
        "col",
        split_axis=0,
        concat_axis=0,
        tiled=True,
    )
    entry_grads = returned.reshape(columns * slot_dev * uniq, width)
    row_list = row_ids.reshape(-1)
    slot_of = jnp.broadcast_to(
        jnp.arange(slot_dev, dtype=jnp.int32)[None, :, None], row_ids.shape
    ).reshape(-1)
    owner = row_list // vocab_dev
    target = slot_of * vocab_dev + row_list % vocab_dev
    span = slot_dev * vocab_dev
    entries = row_list.shape[0]
    capacity = 5 * entries // (4 * owners)
    onehot = (owner[:, None] == jnp.arange(owners, dtype=jnp.int32)).astype(jnp.int32)
    before = jnp.cumsum(onehot, 0) - onehot
    place = jnp.sum(before * onehot, 1)
    target_slot = owner * capacity + place
    bucket = jnp.zeros((owners * capacity, width), jnp.float32).at[target_slot].set(entry_grads)
    labels = (
        jnp.full((owners * capacity,), -1.0, jnp.float32)
        .at[target_slot]
        .set(target.astype(jnp.float32))
    )
    got_rows, got_labels = (
        lax.all_to_all(
            bucket.reshape(owners, capacity, width), "row", split_axis=0, concat_axis=0, tiled=True
        ),
        lax.all_to_all(
            labels.reshape(owners, capacity), "row", split_axis=0, concat_axis=0, tiled=True
        ),
    )
    segment = jnp.where(got_labels >= 0.0, got_labels, float(span)).astype(jnp.int32).reshape(-1)
    summed = jax.ops.segment_sum(got_rows.reshape(-1, width), segment, num_segments=span + 1)[:span]
    row_grads = summed.reshape(slot_dev, vocab_dev, width)
    new_moment1 = 0.9 * moment1 + 0.1 * row_grads
    new_moment2 = 0.99 * moment2 + 0.01 * jnp.mean(row_grads * row_grads, -1)
    row_step = new_moment1 * lax.rsqrt(new_moment2)[..., None]
    return (layer_out, new_moment1, new_moment2, row_step)


def solution(mesh):
    return jax.shard_map(
        body,
        mesh=mesh,
        in_specs=(
            P("row", "col", None),
            P("row", "col", None),
            P("row", "col"),
            P(),
            P(),
            P(None, "row"),
            P("row", None),
            P(),
            P(),
            P(),
            P(("row", "col"), None),
            P("col", "row", None),
            P("col", "row"),
        ),
        out_specs=(
            P(("row", "col"), None),
            P("col", "row", None),
            P("col", "row"),
            P("col", "row", None),
        ),
        check_vma=False,
    )
```

profile of v0, /device:TPU:0, one launch (start us, length us, event | category | flops | bytes accessed | tf_op | source)
XLA Modules:
  0.0 204.6 jit_solution(17181912444277728995)
XLA Ops:
  8.2 13.6 %all_to_all.46 = s32[16,1,128]{2,1,0:T(1,128)S(1)} all-to-all(s32[16,1,128]{2,1,0:T(1,128)S(1)} %reshape.316), channel_id=1, replica_groups=mesh['col'=16,'row'=2] {'col'}, dimensions={0} | all-to-all | bytes 16384 | tf_op jit(solution)/shard_map/all_to_all | solution.py:55
  21.9 3.6 %all-to-all-start.1 = ((bf16[16,8,1536]{2,1,0:T(8,128)(2,1)}), bf16[16,8,1536]{2,1,0:T(8,128)(2,1)S(1)}, u32[]{:S(2)}, u32[]{:S(2)}) async-start(bf16[16,8,1536]{2,1,0:T(8,128)(2,1)} %param.13), calls=%async_computation.1 | async-start | bytes 786432 | tf_op jit(solution)/shard_map/all_to_all | solution.py:59
  28.8 8.7 %all-to-all-done.1 = bf16[16,8,1536]{2,1,0:T(8,128)(2,1)S(1)} async-done(((bf16[16,8,1536]{2,1,0:T(8,128)(2,1)}), bf16[16,8,1536]{2,1,0:T(8,128)(2,1)S(1)}, u32[]{:S(2)}, u32[]{:S(2)}) %all-to-all-start.1) | async-done | bytes 393248 | tf_op jit(solution)/shard_map/all_to_all | solution.py:59
  38.8 2.6 %fusion = bf16[16,128,192]{2,0,1:T(8,128)(2,1)} fusion(bf16[128,8,192]{2,1,0:T(8,128)(2,1)} %reshape.260, s32[16,128]{0,1:T(8,128)} %bitcast_bitcast_fusion.1), kind=kOutput, calls=%fused_computation.7 | convolution fusion | flops 6701056 | bytes 1187840 | tf_op jit(solution)/shard_map/stl,tle->ste/dot_general | solution.py:61
  41.4 2.6 %copy.98 = bf16[16,128,192]{1,2,0:T(8,128)(2,1)} copy(bf16[16,128,192]{2,0,1:T(8,128)(2,1)} %fusion) | data formatting | bytes 1572864 | tf_op jit(solution)/shard_map/convert_element_type | solution.py:61
  50.4 4.6 %all_gather.6 = bf16[32,1024]{1,0:T(8,128)(2,1)S(1)} all-gather(bf16[16,1024]{1,0:T(8,128)(2,1)S(1)} %multiply_convert_fusion.2), channel_id=1, replica_groups=mesh['col'=16,'row'=2] {'row'}, dimensions={0}, use_global_device_ids=true | all-gather | bytes 98304 | tf_op jit(solution)/shard_map/all_gather | solution.py:72
  55.0 2.1 %fusion.48 = f32[32,1024]{1,0:T(8,128)S(1)} fusion(bf16[32,1024]{1,0:T(8,128)(2,1)S(1)} %all_gather.6, bf16[1024,1024]{1,0:T(8,128)(2,1)} %param.18), kind=kOutput, calls=%fused_computation.114 | convolution fusion | flops 67108864 | bytes 2293760 | tf_op jit(solution)/shard_map/dot_general | solution.py:71
  60.9 8.0 %reduce-scatter.3.cloned.1.call-done = f32[16,1536]{1,0:T(8,128)} async-done(((f32[32,1536]{1,0:T(8,128)}), f32[16,1536]{1,0:T(8,128)}) %reduce-scatter.3.cloned.1.call-update) | async-done | bytes 98320 | tf_op jit(solution)/shard_map/reduce_scatter | solution.py:78
  75.0 5.1 %all_gather.7 = bf16[32,1536]{1,0:T(8,128)(2,1)} all-gather(bf16[16,1536]{1,0:T(8,128)(2,1)} %convert_element_type.72), channel_id=1, replica_groups=mesh['col'=16,'row'=2] {'row'}, dimensions={0}, use_global_device_ids=true | all-gather | bytes 147456 | tf_op jit(solution)/shard_map/all_gather | solution.py:93
  80.0 4.0 %convolution_convert_fusion.2 = bf16[32,1024]{1,0:T(8,128)(2,1)} fusion(bf16[1024,1024]{1,0:T(8,128)(2,1)} %param.18, bf16[32,1536]{1,0:T(8,128)(2,1)} %all_gather.7, bf16[1024,1536]{1,0:T(8,128)(2,1)S(1)} %copy-done, f32[32,1024]{1,0:T(8,128)} %copy-done.2), kind=kOutput, calls=%fused_computation.15 | convolution fusion | flops 168099840 | bytes 5537792 | tf_op jit(solution)/shard_map/dot_general | solution.py:101
  84.1 3.5 %fusion.12 = f32[16,192,128]{2,1,0:T(8,128)} fusion(f32[16,16,192]{2,1,0:T(8,128)} %copy-done.4, bf16[8,128]{1,0:T(8,128)(2,1)} %param.20), kind=kOutput, calls=%fused_computation.36 | convolution fusion | flops 37748736 | bytes 1705984 | tf_op jit(solution)/shard_map/lt,sle->ste/dot_general | solution.py:116
  87.6 7.5 %reduce-scatter.5.cloned.1.call-done = bf16[16,1024]{1,0:T(8,128)(2,1)} async-done(((bf16[32,1024]{1,0:T(8,128)(2,1)}), bf16[16,1024]{1,0:T(8,128)(2,1)}) %reduce-scatter.5.cloned.1.call-update) | async-done | bytes 32784 | tf_op jit(solution)/shard_map/reduce_scatter | solution.py:100
  97.7 1.8 copy.107
  99.6 1.8 copy.108
  101.4 2.4 %fusion.50 = f32[16,192,8]{1,2,0:T(8,128)S(1)} fusion(bf16[16,128,192]{1,2,0:T(8,128)(2,1)} %copy.98, f32[16,128,8]{1,2,0:T(8,128)} %copy.108), kind=kOutput, calls=%fused_computation.116 | convolution fusion | flops 37748736 | bytes 950272 | tf_op jit(solution)/shard_map/ste,stk->sek/dot_general | solution.py:110
  103.8 1.9 fusion.49
  108.8 3.0 %copy.111 = f32[16,128,192]{2,0,1:T(8,128)} copy(f32[16,128,192]{1,2,0:T(8,128)} %bitcast_add_fusion) | data formatting | bytes 3145728 | tf_op jit(solution)/shard_map/add | solution.py:119
  111.8 3.5 %fusion.8 = f32[128,8,192]{2,1,0:T(8,128)} fusion(f32[16,128,192]{2,0,1:T(8,128)} %copy.111, s32[16,128]{0,1:T(8,128)S(1)} %copy-done.6), kind=kOutput, calls=%fused_computation.25 | convolution fusion | flops 37765120 | bytes 2367488 | tf_op jit(solution)/shard_map/stl,ste->tle/dot_general | solution.py:122
  115.3 2.4 %reshape.270 = f32[16,8,1536]{2,1,0:T(8,128)} reshape(f32[128,8,192]{2,1,0:T(8,128)} %fusion.8) | data formatting | bytes 1572864 | tf_op jit(solution)/shard_map/reshape | solution.py:124
  117.7 5.8 %all-to-all-start.3 = ((f32[16,8,1536]{2,1,0:T(8,128)}), f32[16,8,1536]{2,1,0:T(8,128)}, u32[]{:S(2)}, u32[]{:S(2)}) async-start(f32[16,8,1536]{2,1,0:T(8,128)} %reshape.270), calls=%async_computation.5 | async-start | bytes 1572864 | tf_op jit(solution)/shard_map/all_to_all | solution.py:123
  125.2 4.3 %scatter_custom_fusion = f32[1280]{0:T(1024)S(1)} fusion(s32[1024]{0:T(1024)S(1)} %bitcast.112, f32[1024]{0:T(1024)S(1)} %get-tuple-element.34, f32[]{:T(128)} %constant.65.clone.1), kind=kCustom, calls=%fused_computation.91 | custom fusion | bytes 5124 | tf_op jit(solution)/shard_map/scatter | solution.py:148
  130.2 12.1 %all-to-all-done.3 = f32[16,8,1536]{2,1,0:T(8,128)} async-done(((f32[16,8,1536]{2,1,0:T(8,128)}), f32[16,8,1536]{2,1,0:T(8,128)}, u32[]{:S(2)}, u32[]{:S(2)}) %all-to-all-start.3) | async-done | bytes 786464 | tf_op jit(solution)/shard_map/all_to_all | solution.py:123
  142.3 3.2 %all-to-all-start.2 = ((f32[2,1,640]{2,1,0:T(1,128)}), f32[2,1,640]{2,1,0:T(1,128)S(1)}, u32[]{:S(2)}, u32[]{:S(2)}) async-start(f32[2,1,640]{2,1,0:T(1,128)} %all_to_all.36), calls=%async_computation.3 | async-start | bytes 10240 | tf_op jit(solution)/shard_map/all_to_all | solution.py:154
  145.5 2.4 %reshape.286 = f32[1024,192]{1,0:T(8,128)} reshape(f32[16,8,1536]{2,1,0:T(8,128)} %all-to-all-done.3) | data formatting | bytes 1572864 | tf_op jit(solution)/shard_map/reshape | solution.py:130
  148.0 6.4 %scatter_custom_fusion.1 = f32[1280,192]{1,0:T(8,128)} fusion(s32[1024]{0:T(1024)S(1)} %bitcast.113, f32[1024,192]{1,0:T(8,128)} %reshape.286, f32[]{:T(128)} %constant.59.clone.1), kind=kCustom, calls=%fused_computation.20 | custom fusion | bytes 983552 | tf_op jit(solution)/shard_map/scatter | solution.py:144
  154.4 2.7 %copy.112 = f32[2,640,192]{1,2,0:T(8,128)} copy(f32[2,640,192]{2,1,0:T(8,128)} %bitcast.105) | data formatting | bytes 1966080 | tf_op jit(solution)/shard_map/reshape | solution.py:152
  157.0 4.4 %all-to-all-start.4 = ((f32[2,640,192]{1,2,0:T(8,128)}), f32[2,640,192]{1,2,0:T(8,128)}, u32[]{:S(2)}, u32[]{:S(2)}) async-start(f32[2,640,192]{1,2,0:T(8,128)} %copy.112), calls=%async_computation.6 | async-start | bytes 1966080 | tf_op jit(solution)/shard_map/all_to_all | solution.py:151
  164.6 10.7 %all-to-all-done.4 = f32[2,640,192]{1,2,0:T(8,128)} async-done(((f32[2,640,192]{1,2,0:T(8,128)}), f32[2,640,192]{1,2,0:T(8,128)}, u32[]{:S(2)}, u32[]{:S(2)}) %all-to-all-start.4) | async-done | bytes 983072 | tf_op jit(solution)/shard_map/all_to_all | solution.py:151
  175.2 2.7 %copy.118 = f32[2,640,192]{2,1,0:T(8,128)} copy(f32[2,640,192]{1,2,0:T(8,128)} %all-to-all-done.4) | data formatting | bytes 1966080 | tf_op jit(solution)/shard_map/reshape | solution.py:159
  177.9 10.5 %scatter_custom_fusion.2 = f32[1025,192]{1,0:T(8,128)} fusion(s32[1280]{0:T(1024)} %fusion.28, f32[1280,192]{1,0:T(8,128)} %bitcast.108, f32[]{:T(128)} %constant.59.clone.1), kind=kCustom, calls=%fused_computation.22 | custom fusion | flops 245760 | bytes 787712 | tf_op jit(solution)/shard_map/scatter-add | solution.py:159
  188.4 2.3 %slice.24 = f32[1024,192]{1,0:T(8,128)} slice(f32[1025,192]{1,0:T(8,128)} %scatter_custom_fusion.2), slice={[0:1024], [0:192]} | slice | bytes 1572864 | tf_op jit(solution)/shard_map/slice | solution.py:159
  190.7 2.4 %copy.120 = f32[1024,192]{0,1:T(8,128)} copy(f32[1024,192]{1,0:T(8,128)} %slice.24) | data formatting | bytes 1572864
  (101 shorter events, 37.5 us)
Async XLA Ops:
  7.2 50.6 %copy-start = (bf16[1024,1536]{1,0:T(8,128)(2,1)S(1)}, bf16[1024,1536]{1,0:T(8,128)(2,1)}, u32[]{:S(2)}) copy-start(bf16[1024,1536]{1,0:T(8,128)(2,1)} %param.19) | copy-start | bytes 9437188
  21.9 15.7 %all-to-all-start.1 = ((bf16[16,8,1536]{2,1,0:T(8,128)(2,1)}), bf16[16,8,1536]{2,1,0:T(8,128)(2,1)S(1)}, u32[]{:S(2)}, u32[]{:S(2)}) async-start(bf16[16,8,1536]{2,1,0:T(8,128)(2,1)} %param.13), calls=%async_computation.1 | async-start | bytes 786432 | tf_op jit(solution)/shard_map/all_to_all | solution.py:59
  25.4 43.5 %reduce-scatter.3.cloned.1.call-start = ((), (), s32[]{:S(2)}) async-start(), calls=%async_computation.7 | async-start | bytes 294912 | tf_op jit(solution)/shard_map/reduce_scatter | solution.py:78
  38.8 5.2 %copy-start.13 = (bf16[128,8]{0,1:T(8,128)(2,1)S(1)}, bf16[128,8]{0,1:T(8,128)(2,1)}, u32[]{:S(2)}) copy-start(bf16[128,8]{0,1:T(8,128)(2,1)} %param.16) | copy-start | bytes 6148
  44.0 6.4 %copy-start.9 = (f32[1024]{0:T(1024)S(1)}, f32[1024]{0:T(1024)}, u32[]{:S(2)}) copy-start(f32[1024]{0:T(1024)} %param.17) | copy-start | bytes 12292
  45.6 0.7 copy-start.7
  47.8 7.2 %copy-start.15 = (f32[16]{0:T(128)}, f32[16]{0:T(128)S(1)}, u32[]{:S(2)}) copy-start(f32[16]{0:T(128)S(1)} %broadcast_multiply_fusion.6) | copy-start | bytes 196
  49.1 5.9 %copy-start.16 = (f32[16]{0:T(128)}, f32[16]{0:T(128)S(1)}, u32[]{:S(2)}) copy-start(f32[16]{0:T(128)S(1)} %add_rsqrt_fusion.1) | copy-start | bytes 196
  50.3 8.7 %copy-start.3 = (f32[16,1024]{1,0:T(8,128)}, f32[16,1024]{1,0:T(8,128)S(1)}, u32[]{:S(2)}) copy-start(f32[16,1024]{1,0:T(8,128)S(1)} %copy.100) | copy-start | bytes 196612
  57.1 0.6 copy-start.2
  57.7 1.4 copy-start.8
  57.7 1.6 copy-start.12
  59.0 36.0 %reduce-scatter.5.cloned.1.call-start = ((), (), s32[]{:S(2)}) async-start(), calls=%async_computation.8 | async-start | bytes 98304 | tf_op jit(solution)/shard_map/reduce_scatter | solution.py:100
  72.1 0.7 copy-start.4
  101.4 4.3 %copy-start.14 = (bf16[128,8]{0,1:T(8,128)(2,1)S(1)}, bf16[128,8]{0,1:T(8,128)(2,1)}, u32[]{:S(2)}) copy-start(bf16[128,8]{0,1:T(8,128)(2,1)} %param.16) | copy-start | bytes 6148
  103.8 3.3 %copy-start.1 = (f32[16,192,128]{2,1,0:T(8,128)S(1)}, f32[16,192,128]{2,1,0:T(8,128)}, u32[]{:S(2)}) copy-start(f32[16,192,128]{2,1,0:T(8,128)} %fusion.12) | copy-start | bytes 4718596
  103.8 3.3 %copy-start.11 = (bf16[16,128]{1,0:T(8,128)(2,1)S(1)}, bf16[16,128]{1,0:T(8,128)(2,1)}, u32[]{:S(2)}) copy-start(bf16[16,128]{1,0:T(8,128)(2,1)} %param.21) | copy-start | bytes 12292
  108.8 3.0 %copy-start.6 = (s32[16,128]{0,1:T(8,128)S(1)}, s32[16,128]{0,1:T(8,128)}, u32[]{:S(2)}) copy-start(s32[16,128]{0,1:T(8,128)} %bitcast_bitcast_fusion.1) | copy-start | bytes 24580
  115.3 8.3 %copy-start.10 = (s32[16,8,8]{0,2,1:T(8,128)S(1)}, s32[16,8,8]{0,2,1:T(8,128)}, u32[]{:S(2)}) copy-start(s32[16,8,8]{0,2,1:T(8,128)} %param.14) | copy-start | bytes 12292
  117.7 24.6 %all-to-all-start.3 = ((f32[16,8,1536]{2,1,0:T(8,128)}), f32[16,8,1536]{2,1,0:T(8,128)}, u32[]{:S(2)}, u32[]{:S(2)}) async-start(f32[16,8,1536]{2,1,0:T(8,128)} %reshape.270), calls=%async_computation.5 | async-start | bytes 1572864 | tf_op jit(solution)/shard_map/all_to_all | solution.py:123
  142.3 14.7 %all-to-all-start.2 = ((f32[2,1,640]{2,1,0:T(1,128)}), f32[2,1,640]{2,1,0:T(1,128)S(1)}, u32[]{:S(2)}, u32[]{:S(2)}) async-start(f32[2,1,640]{2,1,0:T(1,128)} %all_to_all.36), calls=%async_computation.3 | async-start | bytes 10240 | tf_op jit(solution)/shard_map/all_to_all | solution.py:154
  157.0 18.2 %all-to-all-start.4 = ((f32[2,640,192]{1,2,0:T(8,128)}), f32[2,640,192]{1,2,0:T(8,128)}, u32[]{:S(2)}, u32[]{:S(2)}) async-start(f32[2,640,192]{1,2,0:T(8,128)} %copy.112), calls=%async_computation.6 | async-start | bytes 1966080 | tf_op jit(solution)/shard_map/all_to_all | solution.py:151
  193.1 1.5 copy-start.17
  193.1 2.1 %copy-start.5 = (f32[8,128,192]{1,2,0:T(8,128)S(1)}, f32[8,128,192]{1,2,0:T(8,128)}, u32[]{:S(2)}) copy-start(f32[8,128,192]{1,2,0:T(8,128)} %param.24) | copy-start | bytes 2359300
Sparse Core Ops, SparseCore 0:
  59.2 9.7 reduce-scatter.2
  84.2 10.8 reduce-scatter.4
where the time goes:
time: 206 us; the launch traced here: 205 us
  local copies, waits for them, and re-layouts  51.8 us (25%)
  waiting for transfers between devices  47.1 us (23%)
  matrix products  30.7 us (15%)
  blocking collectives  23.3 us (11%)
  other arithmetic  20.3 us (10%)
  starting transfers between devices  17.1 us (8%)
  between operations  14.4 us (7%)
    all_to_all x1, blocking collectives, body(): lax.all_to_all(index_local, 'col', split_axis=0, concat_axis=2, tiled=True)  13.6 us
    all_to_all x1, waiting for transfers between devices, body(): lax.all_to_all(list_grads.reshape(columns, slot_dev, uniq * width), 'col'...  12.1 us
    all_to_all x1, waiting for transfers between devices, body(): lax.all_to_all(bucket.reshape(owners, capacity, width), 'row', split_axis...  10.7 us
    scatter-add x1, other arithmetic, body(): jax.ops.segment_sum(got_rows.reshape(-1, width), segment, num_segments=sp...  10.5 us
    all_to_all x1, waiting for transfers between devices, body(): lax.all_to_all(uniq_rows, 'col', split_axis=0, concat_axis=1, tiled=True)  8.72 us
    reduce_scatter x1, waiting for transfers between devices, body(): lax.psum_scatter(jnp.dot(part_rows, w_down, preferred_element_type=jnp.fl...  8 us
    unnamed x43, local copies, waits for them, and re-layouts  7.56 us
    reduce_scatter x1, waiting for transfers between devices, body(): lax.psum_scatter(lax.dot_general(part_rows, w_up, (((1,), (1,)), ((), ())...  7.52 us
  transfers between devices with their start and end apart: 6, of which 5 were waited for; matrix products, arithmetic and copies ran while one was open for 14% of the time, Pallas kernels for 0%

commit v1 on v0

--- a/solution.py
+++ b/solution.py
@@ -4,6 +4,12 @@
 from jax.sharding import PartitionSpec as P
 
 HIGH = lax.Precision.HIGHEST
+
+
+def exchange_blocks(x, axis, split, join):
+    cells = jnp.split(x, lax.axis_size(axis), axis=split)
+    received = lax.all_to_all(jnp.stack(cells), axis, 0, 0)
+    return jnp.concatenate(received, axis=join)
 
 
 def layer_norm(values, gain):
@@ -52,9 +58,7 @@
     out_rows = w_res.shape[0]
     entry_iota = jnp.arange(uniq, dtype=jnp.int32)
     index_local = sample_idx.reshape(columns, samples, slot_dev)
-    index = lax.all_to_all(index_local, "col", split_axis=0, concat_axis=2, tiled=True).reshape(
-        samples, slots
-    )
+    index = exchange_blocks(index_local, "col", 0, 2).reshape(samples, slots)
     picker = (index[:, :, None] == entry_iota).astype(jnp.bfloat16)
     moved = lax.all_to_all(uniq_rows, "col", split_axis=0, concat_axis=1, tiled=True)
     table = moved.reshape(slots, uniq, width)

time: 206 us -> 218 us (1.058)
  local copies, waits for them, and re-layouts: 51.8 us -> 63.1 us
    unnamed x43 -> x58, local copies, waits for them, and re-layouts: 7.56 us -> 19 us
  transfers between devices with their start and end apart: 6 -> 6, of which waited for: 5 -> 5; matrix products, arithmetic and copies ran while one was open for 14% -> 13% of each run, Pallas kernels for 0% -> 0%
where the time goes in v1:
time: 218 us; the launch traced here: 216 us
  local copies, waits for them, and re-layouts  63.1 us (29%)
  waiting for transfers between devices  47 us (22%)
  matrix products  30.7 us (14%)
  blocking collectives  23.4 us (11%)
  other arithmetic  20.3 us (9%)
  starting transfers between devices  17.1 us (8%)
  between operations  14.4 us (7%)
    unnamed x58, local copies, waits for them, and re-layouts  19 us
    all_to_all x1, blocking collectives, exchange_blocks(): received = lax.all_to_all(jnp.stack(cells), axis, 0, 0)  13.6 us
    all_to_all x1, waiting for transfers between devices, body(): lax.all_to_all(list_grads.reshape(columns, slot_dev, uniq * width), 'col'...  12.1 us
    all_to_all x1, waiting for transfers between devices, body(): lax.all_to_all(bucket.reshape(owners, capacity, width), 'row', split_axis...  10.6 us
    scatter-add x1, other arithmetic, body(): jax.ops.segment_sum(got_rows.reshape(-1, width), segment, num_segments=sp...  10.5 us
    all_to_all x1, waiting for transfers between devices, body(): lax.all_to_all(uniq_rows, 'col', split_axis=0, concat_axis=1, tiled=True)  8.72 us
    reduce_scatter x1, waiting for transfers between devices, body(): lax.psum_scatter(jnp.dot(part_rows, w_down, preferred_element_type=jnp.fl...  8 us
    reduce_scatter x1, waiting for transfers between devices, body(): lax.psum_scatter(lax.dot_general(part_rows, w_up, (((1,), (1,)), ((), ())...  7.49 us
  transfers between devices with their start and end apart: 6, of which 5 were waited for; matrix products, arithmetic and copies ran while one was open for 13% of the time, Pallas kernels for 0%

profile of v1, /device:TPU:0, one launch (start us, length us, event | category | flops | bytes accessed | tf_op | source)
XLA Modules:
  0.0 216.1 jit_solution(14316174603087046279)
XLA Ops:
  19.5 13.6 %all_to_all.36 = s32[16,1,128]{2,1,0:T(1,128)S(1)} all-to-all(s32[16,1,128]{2,1,0:T(1,128)S(1)} %reshape.348), channel_id=1, replica_groups=mesh['col'=16,'row'=2] {'col'}, dimensions={0} | all-to-all | bytes 16384 | tf_op jit(solution)/shard_map/all_to_all | solution.py:11
  33.1 3.6 %all-to-all-start.1 = ((bf16[16,8,1536]{2,1,0:T(8,128)(2,1)}), bf16[16,8,1536]{2,1,0:T(8,128)(2,1)S(1)}, u32[]{:S(2)}, u32[]{:S(2)}) async-start(bf16[16,8,1536]{2,1,0:T(8,128)(2,1)} %param.13), calls=%async_computation.1 | async-start | bytes 786432 | tf_op jit(solution)/shard_map/all_to_all | solution.py:63
  40.1 8.7 %all-to-all-done.1 = bf16[16,8,1536]{2,1,0:T(8,128)(2,1)S(1)} async-done(((bf16[16,8,1536]{2,1,0:T(8,128)(2,1)}), bf16[16,8,1536]{2,1,0:T(8,128)(2,1)S(1)}, u32[]{:S(2)}, u32[]{:S(2)}) %all-to-all-start.1) | async-done | bytes 393248 | tf_op jit(solution)/shard_map/all_to_all | solution.py:63
  50.0 2.6 %fusion = bf16[16,128,192]{2,0,1:T(8,128)(2,1)} fusion(bf16[128,8,192]{2,1,0:T(8,128)(2,1)} %reshape.292, s32[16,128]{0,1:T(8,128)} %bitcast_bitcast_fusion.1), kind=kOutput, calls=%fused_computation.7 | convolution fusion | flops 6701056 | bytes 1187840 | tf_op jit(solution)/shard_map/stl,tle->ste/dot_general | solution.py:65
  52.7 2.6 %copy.93 = bf16[16,128,192]{1,2,0:T(8,128)(2,1)} copy(bf16[16,128,192]{2,0,1:T(8,128)(2,1)} %fusion) | data formatting | bytes 1572864 | tf_op jit(solution)/shard_map/convert_element_type | solution.py:65
  61.7 4.6 %all_gather.6 = bf16[32,1024]{1,0:T(8,128)(2,1)S(1)} all-gather(bf16[16,1024]{1,0:T(8,128)(2,1)S(1)} %multiply_convert_fusion.2), channel_id=1, replica_groups=mesh['col'=16,'row'=2] {'row'}, dimensions={0}, use_global_device_ids=true | all-gather | bytes 98304 | tf_op jit(solution)/shard_map/all_gather | solution.py:76
  66.3 2.1 fusion.48
  72.2 8.0 %reduce-scatter.3.cloned.1.call-done = f32[16,1536]{1,0:T(8,128)} async-done(((f32[32,1536]{1,0:T(8,128)}), f32[16,1536]{1,0:T(8,128)}) %reduce-scatter.3.cloned.1.call-update) | async-done | bytes 98320 | tf_op jit(solution)/shard_map/reduce_scatter | solution.py:82
  86.3 5.2 %all_gather.7 = bf16[32,1536]{1,0:T(8,128)(2,1)} all-gather(bf16[16,1536]{1,0:T(8,128)(2,1)} %convert_element_type.72), channel_id=1, replica_groups=mesh['col'=16,'row'=2] {'row'}, dimensions={0}, use_global_device_ids=true | all-gather | bytes 147456 | tf_op jit(solution)/shard_map/all_gather | solution.py:97
  91.5 4.0 %convolution_convert_fusion.2 = bf16[32,1024]{1,0:T(8,128)(2,1)} fusion(bf16[1024,1024]{1,0:T(8,128)(2,1)} %param.18, bf16[32,1536]{1,0:T(8,128)(2,1)} %all_gather.7, bf16[1024,1536]{1,0:T(8,128)(2,1)S(1)} %copy-done, f32[32,1024]{1,0:T(8,128)} %copy-done.2), kind=kOutput, calls=%fused_computation.15 | convolution fusion | flops 168099840 | bytes 5537792 | tf_op jit(solution)/shard_map/dot_general | solution.py:105
  95.5 3.5 %fusion.12 = f32[16,192,128]{2,1,0:T(8,128)} fusion(f32[16,16,192]{2,1,0:T(8,128)} %copy-done.4, bf16[8,128]{1,0:T(8,128)(2,1)} %param.20), kind=kOutput, calls=%fused_computation.36 | convolution fusion | flops 37748736 | bytes 1705984 | tf_op jit(solution)/shard_map/lt,sle->ste/dot_general | solution.py:120
  99.0 7.5 %reduce-scatter.5.cloned.1.call-done = bf16[16,1024]{1,0:T(8,128)(2,1)} async-done(((bf16[32,1024]{1,0:T(8,128)(2,1)}), bf16[16,1024]{1,0:T(8,128)(2,1)}) %reduce-scatter.5.cloned.1.call-update) | async-done | bytes 32784 | tf_op jit(solution)/shard_map/reduce_scatter | solution.py:104
  109.2 1.8 copy.102
  111.0 1.8 copy.103
  112.8 2.4 %fusion.50 = f32[16,192,8]{1,2,0:T(8,128)S(1)} fusion(bf16[16,128,192]{1,2,0:T(8,128)(2,1)} %copy.93, f32[16,128,8]{1,2,0:T(8,128)} %copy.103), kind=kOutput, calls=%fused_computation.131 | convolution fusion | flops 37748736 | bytes 950272 | tf_op jit(solution)/shard_map/ste,stk->sek/dot_general | solution.py:114
  115.3 1.9 fusion.49
  120.2 3.0 %copy.106 = f32[16,128,192]{2,0,1:T(8,128)} copy(f32[16,128,192]{1,2,0:T(8,128)} %bitcast_add_fusion) | data formatting | bytes 3145728 | tf_op jit(solution)/shard_map/add | solution.py:123
  123.3 3.5 %fusion.8 = f32[128,8,192]{2,1,0:T(8,128)} fusion(f32[16,128,192]{2,0,1:T(8,128)} %copy.106, s32[16,128]{0,1:T(8,128)S(1)} %copy-done.6), kind=kOutput, calls=%fused_computation.25 | convolution fusion | flops 37765120 | bytes 2367488 | tf_op jit(solution)/shard_map/stl,ste->tle/dot_general | solution.py:126
  126.7 2.4 %reshape.302 = f32[16,8,1536]{2,1,0:T(8,128)} reshape(f32[128,8,192]{2,1,0:T(8,128)} %fusion.8) | data formatting | bytes 1572864 | tf_op jit(solution)/shard_map/reshape | solution.py:128
  129.2 5.7 %all-to-all-start.3 = ((f32[16,8,1536]{2,1,0:T(8,128)}), f32[16,8,1536]{2,1,0:T(8,128)}, u32[]{:S(2)}, u32[]{:S(2)}) async-start(f32[16,8,1536]{2,1,0:T(8,128)} %reshape.302), calls=%async_computation.5 | async-start | bytes 1572864 | tf_op jit(solution)/shard_map/all_to_all | solution.py:127
  136.5 4.3 %scatter_custom_fusion = f32[1280]{0:T(1024)S(1)} fusion(s32[1024]{0:T(1024)S(1)} %bitcast.138, f32[1024]{0:T(1024)S(1)} %get-tuple-element.34, f32[]{:T(128)} %constant.65.clone.1), kind=kCustom, calls=%fused_computation.107 | custom fusion | bytes 5124 | tf_op jit(solution)/shard_map/scatter | solution.py:152
  141.4 12.1 %all-to-all-done.3 = f32[16,8,1536]{2,1,0:T(8,128)} async-done(((f32[16,8,1536]{2,1,0:T(8,128)}), f32[16,8,1536]{2,1,0:T(8,128)}, u32[]{:S(2)}, u32[]{:S(2)}) %all-to-all-start.3) | async-done | bytes 786464 | tf_op jit(solution)/shard_map/all_to_all | solution.py:127
  153.6 3.2 %all-to-all-start.2 = ((f32[2,1,640]{2,1,0:T(1,128)}), f32[2,1,640]{2,1,0:T(1,128)S(1)}, u32[]{:S(2)}, u32[]{:S(2)}) async-start(f32[2,1,640]{2,1,0:T(1,128)} %all_to_all.26), calls=%async_computation.3 | async-start | bytes 10240 | tf_op jit(solution)/shard_map/all_to_all | solution.py:158
  156.8 2.4 %reshape.318 = f32[1024,192]{1,0:T(8,128)} reshape(f32[16,8,1536]{2,1,0:T(8,128)} %all-to-all-done.3) | data formatting | bytes 1572864 | tf_op jit(solution)/shard_map/reshape | solution.py:134
  159.2 6.4 %scatter_custom_fusion.1 = f32[1280,192]{1,0:T(8,128)} fusion(s32[1024]{0:T(1024)S(1)} %bitcast.139, f32[1024,192]{1,0:T(8,128)} %reshape.318, f32[]{:T(128)} %constant.59.clone.1), kind=kCustom, calls=%fused_computation.20 | custom fusion | bytes 983552 | tf_op jit(solution)/shard_map/scatter | solution.py:148
  165.6 2.7 %copy.107 = f32[2,640,192]{1,2,0:T(8,128)} copy(f32[2,640,192]{2,1,0:T(8,128)} %bitcast.131) | data formatting | bytes 1966080 | tf_op jit(solution)/shard_map/reshape | solution.py:156
  168.3 4.6 %all-to-all-start.4 = ((f32[2,640,192]{1,2,0:T(8,128)}), f32[2,640,192]{1,2,0:T(8,128)}, u32[]{:S(2)}, u32[]{:S(2)}) async-start(f32[2,640,192]{1,2,0:T(8,128)} %copy.107), calls=%async_computation.6 | async-start | bytes 1966080 | tf_op jit(solution)/shard_map/all_to_all | solution.py:155
  176.0 10.6 %all-to-all-done.4 = f32[2,640,192]{1,2,0:T(8,128)} async-done(((f32[2,640,192]{1,2,0:T(8,128)}), f32[2,640,192]{1,2,0:T(8,128)}, u32[]{:S(2)}, u32[]{:S(2)}) %all-to-all-start.4) | async-done | bytes 983072 | tf_op jit(solution)/shard_map/all_to_all | solution.py:155
  186.7 2.7 %copy.113 = f32[2,640,192]{2,1,0:T(8,128)} copy(f32[2,640,192]{1,2,0:T(8,128)} %all-to-all-done.4) | data formatting | bytes 1966080 | tf_op jit(solution)/shard_map/reshape | solution.py:163
  189.3 10.5 %scatter_custom_fusion.2 = f32[1025,192]{1,0:T(8,128)} fusion(s32[1280]{0:T(1024)} %fusion.28, f32[1280,192]{1,0:T(8,128)} %bitcast.134, f32[]{:T(128)} %constant.59.clone.1), kind=kCustom, calls=%fused_computation.22 | custom fusion | flops 245760 | bytes 787712 | tf_op jit(solution)/shard_map/scatter-add | solution.py:163
  199.8 2.3 %slice.40 = f32[1024,192]{1,0:T(8,128)} slice(f32[1025,192]{1,0:T(8,128)} %scatter_custom_fusion.2), slice={[0:1024], [0:192]} | slice | bytes 1572864 | tf_op jit(solution)/shard_map/slice | solution.py:163
  202.1 2.4 %copy.115 = f32[1024,192]{0,1:T(8,128)} copy(f32[1024,192]{1,0:T(8,128)} %slice.40) | data formatting | bytes 1572864
  (115 shorter events, 48.8 us)
Async XLA Ops:
  7.2 61.8 %copy-start = (bf16[1024,1536]{1,0:T(8,128)(2,1)S(1)}, bf16[1024,1536]{1,0:T(8,128)(2,1)}, u32[]{:S(2)}) copy-start(bf16[1024,1536]{1,0:T(8,128)(2,1)} %param.19) | copy-start | bytes 9437188
  33.1 15.7 %all-to-all-start.1 = ((bf16[16,8,1536]{2,1,0:T(8,128)(2,1)}), bf16[16,8,1536]{2,1,0:T(8,128)(2,1)S(1)}, u32[]{:S(2)}, u32[]{:S(2)}) async-start(bf16[16,8,1536]{2,1,0:T(8,128)(2,1)} %param.13), calls=%async_computation.1 | async-start | bytes 786432 | tf_op jit(solution)/shard_map/all_to_all | solution.py:63
  36.7 43.5 %reduce-scatter.3.cloned.1.call-start = ((), (), s32[]{:S(2)}) async-start(), calls=%async_computation.7 | async-start | bytes 294912 | tf_op jit(solution)/shard_map/reduce_scatter | solution.py:82
  50.0 5.2 %copy-start.13 = (bf16[128,8]{0,1:T(8,128)(2,1)S(1)}, bf16[128,8]{0,1:T(8,128)(2,1)}, u32[]{:S(2)}) copy-start(bf16[128,8]{0,1:T(8,128)(2,1)} %param.16) | copy-start | bytes 6148
  55.3 6.4 %copy-start.9 = (f32[1024]{0:T(1024)S(1)}, f32[1024]{0:T(1024)}, u32[]{:S(2)}) copy-start(f32[1024]{0:T(1024)} %param.17) | copy-start | bytes 12292
  56.9 0.7 copy-start.7
  59.1 7.2 %copy-start.15 = (f32[16]{0:T(128)}, f32[16]{0:T(128)S(1)}, u32[]{:S(2)}) copy-start(f32[16]{0:T(128)S(1)} %broadcast_multiply_fusion.6) | copy-start | bytes 196
  60.4 5.9 %copy-start.16 = (f32[16]{0:T(128)}, f32[16]{0:T(128)S(1)}, u32[]{:S(2)}) copy-start(f32[16]{0:T(128)S(1)} %add_rsqrt_fusion.1) | copy-start | bytes 196
  61.6 8.7 %copy-start.3 = (f32[16,1024]{1,0:T(8,128)}, f32[16,1024]{1,0:T(8,128)S(1)}, u32[]{:S(2)}) copy-start(f32[16,1024]{1,0:T(8,128)S(1)} %copy.95) | copy-start | bytes 196612
  68.4 0.6 copy-start.2
  69.0 1.4 copy-start.8
  69.0 1.6 copy-start.12
  70.3 36.2 %reduce-scatter.5.cloned.1.call-start = ((), (), s32[]{:S(2)}) async-start(), calls=%async_computation.8 | async-start | bytes 98304 | tf_op jit(solution)/shard_map/reduce_scatter | solution.py:104
  83.3 0.7 copy-start.4
  112.8 4.3 %copy-start.14 = (bf16[128,8]{0,1:T(8,128)(2,1)S(1)}, bf16[128,8]{0,1:T(8,128)(2,1)}, u32[]{:S(2)}) copy-start(bf16[128,8]{0,1:T(8,128)(2,1)} %param.16) | copy-start | bytes 6148
  115.3 3.3 %copy-start.1 = (f32[16,192,128]{2,1,0:T(8,128)S(1)}, f32[16,192,128]{2,1,0:T(8,128)}, u32[]{:S(2)}) copy-start(f32[16,192,128]{2,1,0:T(8,128)} %fusion.12) | copy-start | bytes 4718596
  115.3 3.3 %copy-start.11 = (bf16[16,128]{1,0:T(8,128)(2,1)S(1)}, bf16[16,128]{1,0:T(8,128)(2,1)}, u32[]{:S(2)}) copy-start(bf16[16,128]{1,0:T(8,128)(2,1)} %param.21) | copy-start | bytes 12292
  120.2 3.0 %copy-start.6 = (s32[16,128]{0,1:T(8,128)S(1)}, s32[16,128]{0,1:T(8,128)}, u32[]{:S(2)}) copy-start(s32[16,128]{0,1:T(8,128)} %bitcast_bitcast_fusion.1) | copy-start | bytes 24580
  126.7 8.1 %copy-start.10 = (s32[16,8,8]{0,2,1:T(8,128)S(1)}, s32[16,8,8]{0,2,1:T(8,128)}, u32[]{:S(2)}) copy-start(s32[16,8,8]{0,2,1:T(8,128)} %param.14) | copy-start | bytes 12292
  129.2 24.4 %all-to-all-start.3 = ((f32[16,8,1536]{2,1,0:T(8,128)}), f32[16,8,1536]{2,1,0:T(8,128)}, u32[]{:S(2)}, u32[]{:S(2)}) async-start(f32[16,8,1536]{2,1,0:T(8,128)} %reshape.302), calls=%async_computation.5 | async-start | bytes 1572864 | tf_op jit(solution)/shard_map/all_to_all | solution.py:127
  153.6 14.7 %all-to-all-start.2 = ((f32[2,1,640]{2,1,0:T(1,128)}), f32[2,1,640]{2,1,0:T(1,128)S(1)}, u32[]{:S(2)}, u32[]{:S(2)}) async-start(f32[2,1,640]{2,1,0:T(1,128)} %all_to_all.26), calls=%async_computation.3 | async-start | bytes 10240 | tf_op jit(solution)/shard_map/all_to_all | solution.py:158
  168.3 18.4 %all-to-all-start.4 = ((f32[2,640,192]{1,2,0:T(8,128)}), f32[2,640,192]{1,2,0:T(8,128)}, u32[]{:S(2)}, u32[]{:S(2)}) async-start(f32[2,640,192]{1,2,0:T(8,128)} %copy.107), calls=%async_computation.6 | async-start | bytes 1966080 | tf_op jit(solution)/shard_map/all_to_all | solution.py:155
  204.5 1.5 copy-start.17
  204.5 2.1 copy-start.5
Sparse Core Ops, SparseCore 0:
  70.4 9.7 reduce-scatter.2
  95.7 10.8 reduce-scatter.4
